TPU v7x, 32 devices: a whole 2x2x4 slice. The times are simulated.
32 devices in a mesh: row: 4 (over y, x), col: 8 (over z, core).
Axes of the slice: x: 2, y: 2, z: 4, core: 2. Of those that a mesh axis runs over, the one named last changes fastest.
Arguments:
- root_inverse: float32 [12288, 12288], P('row', 'col'), may hold values from -6 to 6, as said below
- panel_root: float32 [2, 12288, 256], P(None, ('row', 'col')), may hold values from -0.0546875 to 0.0546875
- panel_tail: float32 [1, 256, 256], replicated, may hold values from -0.375 to 0.375
- factor_inverse: float32 [2, 256, 256], replicated, may hold values from -1 to 2, as said below
- ancestors: int32 [84], replicated, may hold values from 0 to 95, as said below
Outputs:
- border: float32 [2, 12288, 256], P(None, ('row', 'col'))
- border_tail: float32 [1, 256, 256], replicated
- diagonal: float32 [2, 256, 256], replicated
Inputs may be any that keep to these rules, and one draw needn't show every extreme that they name: `ancestors`: each of the two lists is increasing and holds distinct root blocks; the list of supernode 1 is a subset of that of supernode 0. `factor_inverse`: each block is lower triangular with a positive diagonal. `root_inverse`: the matrix is symmetric.
All inputs are finite; a program needn't handle non-finite values.
Results may differ from a plain program's by a relative error of at most 0.0001.
Values sent between devices are 32-bit elements; how exact they have to be, the bound alone decides.
No kernel may reach another device: no remote copies, remote signals or barrier semaphores. Data moves between devices by JAX's collectives and lax.ppermute only.
A program may use at most 64 MiB of HBM per device.

v0:
```python
import jax
import jax.numpy as jnp
from jax import lax
from jax.sharding import PartitionSpec as P

R = 12288
BLK = 128


def from_root(x, axis, root):
    mine = lax.axis_index(axis) == root
    return lax.psum(jnp.where(mine, x, jnp.zeros_like(x)), axis)


def product(left, right):
    return jnp.dot(left, right, precision=lax.Precision.HIGHEST, preferred_element_type=jnp.float32)


def tail_slot(later, earlier):
    return later * (later - 1) // 2 + earlier


def member(start, count, listed):
    block_ids = (start + lax.iota(jnp.int32, count)) // BLK
    return jnp.any(block_ids[:, None] == listed[None, :], axis=1).astype(jnp.float32)[:, None]


def local(root_inverse, panel_root, panel_tail, factor_inverse, ancestors):
    row_index = lax.axis_index("row")
    col_index = lax.axis_index("col")
    share = panel_root.shape[1]
    block_rows = root_inverse.shape[0]
    col_rows = root_inverse.shape[1]
    share_start = row_index * block_rows + col_index * share
    nblocks = R // BLK
    counts = [nblocks // 2, 3 * nblocks // 8]
    lists = []
    start = 0
    for node in range(2):
        lists.append(ancestors[start : start + counts[node]])
        start = start + counts[node]
    borders = []
    diagonals = []
    tails = [None]
    for node in range(2):
        listed = lists[node]
        gathered = lax.all_gather(panel_root[node : node + 1], "col", axis=1, tiled=True)
        owner = col_index * col_rows // block_rows
        offset = col_index * col_rows - owner * block_rows
        column_part = lax.dynamic_slice_in_dim(gathered, offset, col_rows, 1)
        column_part = from_root(column_part, "row", owner)
        col_start = col_index * col_rows
        joined = [column_part[0] * member(col_start, col_rows, [listed][0])][0]
        images = lax.psum_scatter(
            product(root_inverse, joined), "col", scatter_dimension=0, tiled=True
        )
        image = [images][0]
        mask = member(share_start, share, listed)
        panel = panel_root[node] * mask
        for prior in range(node):
            image = image + product(borders[prior], panel_tail[tail_slot(node, prior)])
        crossing = [product(borders[prior].T, panel) for prior in range(node)]
        carried = []
        for prior in range(node):
            value = product(diagonals[prior], panel_tail[tail_slot(node, 0)])
            carried.append(value)
        own_part = product(panel.T, image)
        base = product(factor_inverse[node].T, factor_inverse[node])
        cross = []
        joint = own_part
        for prior in range(node):
            joint = joint + product(panel_tail[tail_slot(node, prior)].T, crossing[prior])
        totals = lax.psum(tuple([joint] + crossing), ("row", "col"))
        block = base + totals[0]
        for prior in range(node):
            cross.append(totals[1 + prior] + carried[prior])
            block = block + product(panel_tail[tail_slot(node, prior)].T, carried[prior])
        for prior in range(node):
            tails[tail_slot(node, prior)] = -cross[prior]
        borders.append(-(mask * image))
        diagonals.append(block)
    return (jnp.stack(borders), jnp.stack(tails), jnp.stack(diagonals))


def solution(mesh):
    placed = (P("row", "col"), P(None, ("row", "col"), None), P(), P(), P())
    return jax.shard_map(
        local,
        mesh=mesh,
        in_specs=placed,
        out_specs=(P(None, ("row", "col"), None), P(), P()),
        check_vma=False,
    )
```

profile of v0, /device:TPU:0, one launch (start us, length us, event | category | flops | bytes accessed | tf_op | source)
XLA Modules:
  0.0 430.4 jit_solution(5512054418208885752)
XLA Ops:
  7.2 1.2 fusion.31
  8.4 0.9 copy.23
  9.4 0.9 copy.24
  10.4 40.7 %all-gather.3.cloned.1.call-done = f32[1,3072,256]{1,2,0:T(8,128)} async-done(((f32[1,384,256]{1,2,0:T(8,128)}), f32[1,3072,256]{1,2,0:T(8,128)}) %all-gather.3.cloned.1.call-update) | async-done | bytes 3145744 | tf_op jit(solution)/shard_map/all_gather | solution.py:47
  51.1 2.7 select_bitcast_fusion.1
  53.8 36.7 %all-gather.5.cloned.1.call-done = f32[1,3072,256]{1,2,0:T(8,128)} async-done(((f32[1,384,256]{1,2,0:T(8,128)}), f32[1,3072,256]{1,2,0:T(8,128)}) %all-gather.5.cloned.1.call-update) | async-done | bytes 3145744 | tf_op jit(solution)/shard_map/all_gather | solution.py:47
  90.5 2.7 select_bitcast_fusion
  94.0 85.5 %all-reduce.7.cloned.1.call-done = (f32[1536,256]{0,1:T(8,128)}, f32[1536,256]{0,1:T(8,128)}) async-done(((f32[1536,256]{0,1:T(8,128)}, f32[1536,256]{0,1:T(8,128)}), (f32[1536,256]{0,1:T(8,128)}, f32[1536,256]{0,1:T(8,128)})) %all-reduce.7.cloned.1.call-update) | async-done | bytes 3145744 | tf_op jit(solution)/shard_map/psum | solution.py:12
  179.5 20.6 %convolution_bitcast_fusion.1 = f32[3072,256]{0,1:T(8,128)} fusion(f32[3072,1536]{1,0:T(8,128)} %param.5, f32[1536,256]{0,1:T(8,128)} %get-tuple-element.13, f32[1536]{0:T(1024)S(1)} %convert_element_type.29), kind=kOutput, calls=%fused_computation.1 | convolution fusion | flops 14495907840 | bytes 23599104 | tf_op jit(solution)/shard_map/dot_general | solution.py:16
  200.3 1.1 copy-done.4
  201.5 20.1 %convolution_bitcast_fusion = f32[3072,256]{0,1:T(8,128)} fusion(f32[3072,1536]{1,0:T(8,128)} %param.5, f32[1536,256]{0,1:T(8,128)S(1)} %copy-done.4, f32[1536]{0:T(1024)S(1)} %convert_element_type.31), kind=kOutput, calls=%fused_computation | convolution fusion | flops 14495907840 | bytes 23599104 | tf_op jit(solution)/shard_map/dot_general | solution.py:16
  222.1 18.5 %reduce-scatter.3.cloned.1.call-done = f32[384,256]{0,1:T(8,128)} async-done(((f32[3072,256]{0,1:T(8,128)}), f32[384,256]{0,1:T(8,128)}) %reduce-scatter.3.cloned.1.call-update) | async-done | bytes 393232 | tf_op jit(solution)/shard_map/reduce_scatter | solution.py:54
  240.6 41.8 %reduce-scatter.5.cloned.1.call-done = f32[384,256]{0,1:T(8,128)} async-done(((f32[3072,256]{0,1:T(8,128)}), f32[384,256]{0,1:T(8,128)}) %reduce-scatter.5.cloned.1.call-update) | async-done | bytes 393232 | tf_op jit(solution)/shard_map/reduce_scatter | solution.py:54
  282.5 1.8 convolution_add_fusion
  284.2 0.6 fusion.8
  284.9 0.6 fusion.9
  285.5 1.3 fusion.4
  286.8 1.3 fusion.7
  288.3 1.1 copy.19
  289.5 129.3 %all-reduce.5.cloned.1.call-done = (f32[256,256]{1,0:T(8,128)}, f32[256,256]{1,0:T(8,128)}, f32[256,256]{1,0:T(8,128)}) async-done(((f32[256,256]{1,0:T(8,128)}, f32[256,256]{1,0:T(8,128)}, f32[256,256]{1,0:T(8,128)}), (f32[256,256]{1,0:T(8,128)}, f32[256,256]{1,0:T(8,128)}, f32[256,256]{1,0:T(8,128)})) %all-reduce.5.cloned.1.call-update) | async-done | bytes 786448 | tf_op jit(solution)/shard_map/psum | solution.py:73
  418.7 1.6 convolution_add_fusion.2
  421.3 0.6 fusion.3
  422.0 0.7 negate_bitcast_fusion.1
  422.7 0.8 pad_maximum_fusion.1
  (47 shorter events, 2.8 us)
Async XLA Ops:
  7.2 275.3 %copy-start = (f32[1,256,256]{2,1,0:T(8,128)S(1)}, f32[1,256,256]{2,1,0:T(8,128)}, u32[]{:S(2)}) copy-start(f32[1,256,256]{2,1,0:T(8,128)} %param.7) | copy-start | bytes 786436
  7.2 44.0 %all-gather.3.cloned.1.call-start = ((), (), s32[]{:S(2)}) async-start(), calls=%async_computation.2 | async-start | bytes 3538944 | tf_op jit(solution)/shard_map/all_gather | solution.py:47
  9.4 81.1 %all-gather.5.cloned.1.call-start = ((), (), s32[]{:S(2)}) async-start(), calls=%async_computation.4 | async-start | bytes 3538944 | tf_op jit(solution)/shard_map/all_gather | solution.py:47
  10.4 169.1 %all-reduce.7.cloned.1.call-start = ((), (), s32[]{:S(2)}) async-start(), calls=%async_computation.7 | async-start | bytes 6291456 | tf_op jit(solution)/shard_map/psum | solution.py:12
  93.2 0.7 copy-start.9
  93.2 147.4 %reduce-scatter.3.cloned.1.call-start = ((), (), s32[]{:S(2)}) async-start(), calls=%async_computation.3 | async-start | bytes 3538944 | tf_op jit(solution)/shard_map/reduce_scatter | solution.py:54
  200.1 1.4 copy-start.4
  200.1 82.4 %reduce-scatter.5.cloned.1.call-start = ((), (), s32[]{:S(2)}) async-start(), calls=%async_computation.5 | async-start | bytes 3538944 | tf_op jit(solution)/shard_map/reduce_scatter | solution.py:54
  221.6 62.6 %copy-start.1 = (f32[1,384,256]{1,2,0:T(8,128)S(1)}, f32[1,384,256]{1,2,0:T(8,128)}, u32[]{:S(2)}) copy-start(f32[1,384,256]{1,2,0:T(8,128)} %copy.24) | copy-start | bytes 1179652
  221.7 197.1 %all-reduce.5.cloned.1.call-start = ((), (), s32[]{:S(2)}) async-start(), calls=%async_computation.6 | async-start | bytes 1572864 | tf_op jit(solution)/shard_map/psum | solution.py:73
  240.6 44.2 %copy-start.2 = (f32[384,256]{0,1:T(8,128)S(1)}, f32[384,256]{0,1:T(8,128)}, u32[]{:S(2)}) copy-start(f32[384,256]{0,1:T(8,128)} %reduce-scatter.3.cloned.1.call-done) | copy-start | bytes 1179652
  284.2 2.6 copy-start.3
  285.5 2.6 copy-start.5
  288.2 130.5 %copy-start.6 = (f32[2,256,256]{2,1,0:T(8,128)S(1)}, f32[2,256,256]{2,1,0:T(8,128)}, u32[]{:S(2)}) copy-start(f32[2,256,256]{2,1,0:T(8,128)} %param.8) | copy-start | bytes 1572868
  418.7 2.0 copy-start.8
  418.7 3.2 copy-start.7
Sparse Core Ops, SparseCore 0:
  10.2 40.9 all-gather.2
  53.3 37.1 all-gather.4
  93.6 85.8 all-reduce.6
  200.2 40.3 reduce-scatter.2
  242.8 39.6 reduce-scatter.4
  288.4 130.2 all-reduce.4
where the time goes:
time: 431 us; the launch traced here: 430 us
  waiting for transfers between devices  353 us (82%)
  matrix products  49.5 us (11%)
  between operations  14.3 us (3%)
  other arithmetic  7.57 us (2%)
  local copies, waits for them, and re-layouts  5.99 us (1%)
    psum x1, waiting for transfers between devices, local(): totals = lax.psum(tuple([joint] + crossing), ('row', 'col'))  129 us
    psum x1, waiting for transfers between devices, from_root(): return lax.psum(jnp.where(mine, x, jnp.zeros_like(x)), axis)  85.5 us
    all_gather x2, waiting for transfers between devices, local(): lax.all_gather(panel_root[node:node + 1], 'col', axis=1, tiled=True)  77.4 us
    reduce_scatter x2, waiting for transfers between devices, local(): lax.psum_scatter(product(root_inverse, joined), 'col', scatter_dimension=...  60.3 us
    dot_general x11, matrix products, product(): jnp.dot(left, right, precision=lax.Precision.HIGHEST, preferred_element_t...  49.5 us
  transfers between devices with their start and end apart: 6, of which 6 were waited for; matrix products, arithmetic and copies ran while one was open for 6% of the time, Pallas kernels for 0%

commit v1 on v0

v1 whole, which is shorter than its diff:
```python
import jax
import jax.numpy as jnp
from jax import lax
from jax.sharding import PartitionSpec as P

BLK = 128


def product(left, right, precision=lax.Precision.HIGHEST):
    return jnp.dot(left, right, precision=precision, preferred_element_type=jnp.float32)


def over_rows(left, right, precision=lax.Precision.HIGHEST):
    return lax.dot_general(
        left, right, (((0,), (0,)), ((), ())), precision=precision, preferred_element_type=jnp.float32
    )


def member(start, count, listed):
    block_ids = (start + lax.iota(jnp.int32, count)) // BLK
    return jnp.any(block_ids[:, None] == listed[None, :], axis=1).astype(jnp.float32)[:, None]


def tree_sum(parts):
    while len(parts) > 1:
        parts = [parts[k] + parts[k + 1] for k in range(0, len(parts), 2)]
    return parts[0]


def pick(index, parts):
    value = parts[0]
    for k in range(1, len(parts)):
        value = jnp.where(index == k, parts[k], value)
    return value


class Slice:
    def __init__(self, mesh):
        self.rows = mesh.shape["row"]
        self.cols = mesh.shape["col"]
        self.planes = self.cols // 2

    def across(self, x, step):
        return lax.ppermute(x, "row", [(r, r ^ step) for r in range(self.rows)])

    def swap(self, x):
        return lax.ppermute(x, "col", [(c, c ^ 1) for c in range(self.cols)])

    def along(self, x, step):
        return lax.ppermute(x, "col", [(c, c ^ (2 * step)) for c in range(self.cols)])

    def up(self, x, step):
        pairs = [(2 * z + c, 2 * z + 2 + c) for z in range(step - 1, self.planes - 1) for c in (0, 1)]
        return lax.ppermute(x, "col", pairs)

    def down(self, x, step):
        pairs = [(2 * z + c, 2 * z - 2 + c) for z in range(1, self.planes - step + 1) for c in (0, 1)]
        return lax.ppermute(x, "col", pairs)

    def home(self, x):
        pairs = []
        for r in range(self.rows):
            for c in range(self.cols):
                pairs.append((r * self.cols + c, self.rows * c + r))
        return lax.ppermute(x, ("row", "col"), pairs)


def gather_block(net, x, plane, core):
    rising, falling = [x], [x]
    for step in range(1, net.planes):
        rising.append(net.up(rising[-1], step))
        falling.append(net.down(falling[-1], step))
    mine = [x] + [rising[d] + falling[net.planes - d] for d in range(1, net.planes)]
    other = [net.swap(piece) for piece in mine]
    first = [jnp.where(core == 0, a, b) for a, b in zip(mine, other)]
    second = [jnp.where(core == 0, b, a) for a, b in zip(mine, other)]
    pairs = [jnp.concatenate([a, b], axis=0) for a, b in zip(first, second)]
    size = pairs[0].shape[0]
    backward = jnp.concatenate([pairs[(net.planes - k) % net.planes] for k in range(net.planes)] * 2, axis=0)
    start = lax.rem(net.planes - plane, net.planes) * size
    return lax.dynamic_slice_in_dim(backward, start, net.planes * size, 0)


def reduce_rows(net, x, row):
    size = x.shape[0] // net.rows
    parts = [lax.dynamic_slice_in_dim(x, row * size, size, 0)]
    for step in range(1, net.rows):
        parts.append(net.across(lax.dynamic_slice_in_dim(x, (row ^ step) * size, size, 0), step))
    return tree_sum(parts)


def reduce_all(net, x, row, core):
    half = x.shape[0] // 2
    low, high = x[:half], x[half:]
    mine = jnp.where(core == 0, low, high) + net.swap(jnp.where(core == 0, high, low))
    part = reduce_rows(net, mine, row)
    part = tree_sum([part] + [net.along(part, step) for step in range(1, net.planes)])
    got = [part] + [net.across(part, step) for step in range(1, net.rows)]
    mine = jnp.concatenate(
        [pick(row, [got[r ^ at] for r in range(net.rows)]) for at in range(net.rows)], axis=0
    )
    other = net.swap(mine)
    return jnp.concatenate(
        [jnp.where(core == 0, mine, other), jnp.where(core == 0, other, mine)], axis=0
    )


def solution(mesh):
    net = Slice(mesh)
    placed = (P("row", "col"), P(None, ("row", "col"), None), P(), P(), P())

    def local(root_inverse, panel_root, panel_tail, factor_inverse, ancestors):
        row = lax.axis_index("row")
        col = lax.axis_index("col")
        plane, core = col // 2, col % 2
        share, width = panel_root.shape[1:]
        block_rows = root_inverse.shape[0]
        nblocks = block_rows * net.rows // BLK
        count = nblocks // 2
        start = row * block_rows + col * share
        masks = [
            member(start, share, ancestors[:count]),
            member(start, share, ancestors[count:]),
        ]
        panels = [panel_root[k] * masks[k] for k in range(2)]
        tail = panel_tail[0]
        images = []
        for k in range(2):
            whole = gather_block(net, panels[k], plane, core)
            partial = over_rows(root_inverse, whole, lax.Precision.HIGH)
            images.append(net.home(reduce_rows(net, partial, row)))
        first = -(masks[0] * images[0])
        second = images[1] + product(first, tail)
        own0 = over_rows(panels[0], images[0])
        cross = over_rows(first, panels[1])
        own1 = over_rows(panels[1], second) + over_rows(tail, cross)
        total = reduce_all(net, jnp.concatenate([own0, cross, own1], axis=0), row, core)
        block0 = over_rows(factor_inverse[0], factor_inverse[0]) + total[:width]
        carried = product(block0, tail)
        crossed = total[width : 2 * width] + carried
        block1 = (
            over_rows(factor_inverse[1], factor_inverse[1])
            + total[2 * width :]
            + over_rows(tail, carried)
        )
        border = jnp.stack([first, -(masks[1] * second)])
        return border, -crossed[None], jnp.stack([block0, block1])

    return jax.shard_map(
        local,
        mesh=mesh,
        in_specs=placed,
        out_specs=(P(None, ("row", "col"), None), P(), P()),
        check_vma=False,
    )
```

time: 431 us -> 223 us (0.52)
  waiting for transfers between devices: 353 us -> 78.9 us
  starting transfers between devices: 0.43 us -> 53 us
  other arithmetic: 7.57 us -> 46.2 us
  matrix products: 49.5 us -> 34.5 us
  between operations: 14.3 us -> 1.19 us
    psum x2 -> x0, waiting for transfers between devices: 215 us -> none  [the longest x1 129 us: local(): totals = lax.psum(tuple([joint] + crossing), ('row', 'col'))]
    ppermute x0 -> x39, waiting for transfers between devices: none -> 78.9 us  [the longest x12 33.7 us: across(): return lax.ppermute(x, 'row', [(r, r ^ step) for r in range(self.rows)])]
    all_gather x2 -> x0, waiting for transfers between devices: 77.4 us -> none  [local(): lax.all_gather(panel_root[node:node + 1], 'col', axis=1, tiled=True)]
    reduce_scatter x2 -> x0, waiting for transfers between devices: 60.3 us -> none  [local(): lax.psum_scatter(product(root_inverse, joined), 'col', scatter_dimension=...]
    ppermute x0 -> x39, starting transfers between devices: none -> 53 us  [the longest x12 19.9 us: across(): return lax.ppermute(x, 'row', [(r, r ^ step) for r in range(self.rows)])]
    unnamed x0 -> x30, other arithmetic: none -> 32.2 us
    dot_general x11, matrix products: 49.5 us -> 34.5 us  [the longest x9 33.2 us: over_rows(): lax.dot_general(left, right, (((0,), (0,)), ((), ())), precision=precisio...]
    add x0 -> x11, other arithmetic: none -> 8.63 us  [the longest x6 6.16 us: gather_block(): rising[d] + falling[net.planes - d]]
  transfers between devices with their start and end apart: 6 -> 39, of which waited for: 6 -> 20; matrix products, arithmetic and copies ran while one was open for 6% -> 36% of each run, Pallas kernels for 0% -> 0%
where the time goes in v1:
time: 223 us; the launch traced here: 222 us
  waiting for transfers between devices  78.9 us (35%)
  starting transfers between devices  53 us (24%)
  other arithmetic  46.2 us (21%)
  matrix products  34.5 us (15%)
  local copies, waits for them, and re-layouts  8.18 us (4%)
    ppermute x12, waiting for transfers between devices, across(): return lax.ppermute(x, 'row', [(r, r ^ step) for r in range(self.rows)])  33.7 us
    dot_general x9, matrix products, over_rows(): lax.dot_general(left, right, (((0,), (0,)), ((), ())), precision=precisio...  33.2 us
    unnamed x30, other arithmetic  32.2 us
    ppermute x6, waiting for transfers between devices, down(): return lax.ppermute(x, 'col', pairs)  26.5 us
    ppermute x12, starting transfers between devices, across(): return lax.ppermute(x, 'row', [(r, r ^ step) for r in range(self.rows)])  19.9 us
    ppermute x6, starting transfers between devices, up(): return lax.ppermute(x, 'col', pairs)  11.9 us
    ppermute x3, waiting for transfers between devices, along(): return lax.ppermute(x, 'col', [(c, c ^ 2 * step) for c in range(self.cols)])  8.58 us
    ppermute x6, waiting for transfers between devices, up(): return lax.ppermute(x, 'col', pairs)  8.15 us
  transfers between devices with their start and end apart: 39, of which 20 were waited for; matrix products, arithmetic and copies ran while one was open for 36% of the time, Pallas kernels for 0%

profile of v1, /device:TPU:0, one launch (start us, length us, event | category | flops | bytes accessed | tf_op | source)
XLA Modules:
  0.0 221.9 jit_solution(2150986868224283674)
XLA Ops:
  2.9 5.0 %collective-permute-start.1 = (f32[384,256]{0,1:T(8,128)S(1)}, f32[384,256]{0,1:T(8,128)S(1)}, u32[]{:S(2)}, u32[]{:S(2)}) collective-permute-start(f32[384,256]{0,1:T(8,128)S(1)} %bitcast_multiply_fusion.1), channel_id=1, source_target_pairs={{0,2},{1,3},{2,4},{3,5},{4,6},{5,7},{8,10},{9,11},{10,12},{11,13},... | collective-permute-start | bytes 1179656 | tf_op jit(solution)/shard_map/ppermute | solution.py:54
  9.0 3.5 %collective-permute-start.15 = (f32[384,256]{0,1:T(8,128)S(1)}, f32[384,256]{0,1:T(8,128)S(1)}, u32[]{:S(2)}, u32[]{:S(2)}) collective-permute-start(f32[384,256]{0,1:T(8,128)S(1)} %bitcast_multiply_fusion), channel_id=1, source_target_pairs={{0,2},{1,3},{2,4},{3,5},{4,6},{5,7},{8,10},{9,11},{10,12},{11,13},... | collective-permute-start | bytes 1179656 | tf_op jit(solution)/shard_map/ppermute | solution.py:54
  15.1 2.2 %collective-permute-done.1 = f32[384,256]{0,1:T(8,128)S(1)} collective-permute-done((f32[384,256]{0,1:T(8,128)S(1)}, f32[384,256]{0,1:T(8,128)S(1)}, u32[]{:S(2)}, u32[]{:S(2)}) %collective-permute-start.1) | collective-permute-done | bytes 393248 | tf_op jit(solution)/shard_map/ppermute | solution.py:54
  18.7 5.9 %collective-permute-done.15 = f32[384,256]{0,1:T(8,128)S(1)} collective-permute-done((f32[384,256]{0,1:T(8,128)S(1)}, f32[384,256]{0,1:T(8,128)S(1)}, u32[]{:S(2)}, u32[]{:S(2)}) %collective-permute-start.15) | collective-permute-done | bytes 393248 | tf_op jit(solution)/shard_map/ppermute | solution.py:54
  27.7 7.1 %collective-permute-done.4 = f32[384,256]{0,1:T(8,128)} collective-permute-done((f32[384,256]{0,1:T(8,128)S(1)}, f32[384,256]{0,1:T(8,128)}, u32[]{:S(2)}, u32[]{:S(2)}) %collective-permute-start.4) | collective-permute-done | bytes 393248 | tf_op jit(solution)/shard_map/ppermute | solution.py:58
  39.2 4.6 %collective-permute-done.20 = f32[384,256]{0,1:T(8,128)S(1)} collective-permute-done((f32[384,256]{0,1:T(8,128)}, f32[384,256]{0,1:T(8,128)S(1)}, u32[]{:S(2)}, u32[]{:S(2)}) %collective-permute-start.20) | collective-permute-done | bytes 393248 | tf_op jit(solution)/shard_map/ppermute | solution.py:58
  45.1 7.1 %collective-permute-done.6 = f32[384,256]{0,1:T(8,128)S(1)} collective-permute-done((f32[384,256]{0,1:T(8,128)}, f32[384,256]{0,1:T(8,128)S(1)}, u32[]{:S(2)}, u32[]{:S(2)}) %collective-permute-start.6) | collective-permute-done | bytes 393248 | tf_op jit(solution)/shard_map/ppermute | solution.py:58
  62.0 5.8 %collective-permute-done.8 = f32[384,256]{0,1:T(8,128)S(1)} collective-permute-done((f32[384,256]{0,1:T(8,128)S(1)}, f32[384,256]{0,1:T(8,128)S(1)}, u32[]{:S(2)}, u32[]{:S(2)}) %collective-permute-start.8) | collective-permute-done | bytes 393248 | tf_op jit(solution)/shard_map/ppermute | solution.py:58
  81.0 16.3 %fusion.2 = f32[256,1536]{1,0:T(8,128)} fusion(f32[3072,1536]{1,0:T(8,128)S(1)} %copy-done.1, f32[6144,256]{0,1:T(8,128)} %fusion.48, s32[]{:T(128)S(6)} %select_n.205), kind=kOutput, calls=%fused_computation.2 | convolution fusion | flops 7247757312 | bytes 23592964 | tf_op jit(solution)/shard_map/dot_general | solution.py:14
  97.3 2.3 %dynamic-slice_bitcast_fusion.3 = (f32[384,256]{0,1:T(8,128)}, f32[384,256]{0,1:T(8,128)}, f32[384,256]{0,1:T(8,128)}) fusion(f32[256,1536]{1,0:T(8,128)} %fusion.2, s32[]{:T(128)S(6)} %select_n.209, s32[]{:T(128)S(6)} %select_n.208, s32[]{:T(128)S(6)} %select_n.207), kind=kLoop, calls=%fused_computation.24 | loop fusion | bytes 2359308 | tf_op jit(solution)/shard_map/dynamic_slice | solution.py:88
  104.9 1.9 fusion.55
  110.3 1.9 fusion.63
  113.8 1.9 fusion.54
  118.5 1.9 fusion.60
  123.0 11.7 %fusion = f32[256,1536]{1,0:T(8,128)S(1)} fusion(f32[3072,1536]{1,0:T(8,128)S(1)} %copy-done.1, f32[6144,256]{0,1:T(8,128)} %fusion.64, s32[]{:T(128)S(6)} %select_n.205), kind=kOutput, calls=%fused_computation | convolution fusion | flops 7247757312 | bytes 23592964 | tf_op jit(solution)/shard_map/dot_general | solution.py:14
  140.5 7.8 %collective-permute-done.24 = f32[384,256]{0,1:T(8,128)S(1)} collective-permute-done((f32[384,256]{0,1:T(8,128)S(1)}, f32[384,256]{0,1:T(8,128)S(1)}, u32[]{:S(2)}, u32[]{:S(2)}) %collective-permute-start.24) | collective-permute-done | bytes 393248 | tf_op jit(solution)/shard_map/ppermute | solution.py:44
  148.3 13.9 %collective-permute-done.25 = f32[384,256]{0,1:T(8,128)S(1)} collective-permute-done((f32[384,256]{0,1:T(8,128)S(1)}, f32[384,256]{0,1:T(8,128)S(1)}, u32[]{:S(2)}, u32[]{:S(2)}) %collective-permute-start.25) | collective-permute-done | bytes 393248 | tf_op jit(solution)/shard_map/ppermute | solution.py:44
  170.4 6.2 %collective-permute-start.28 = (f32[384,256]{0,1:T(8,128)S(1)}, f32[384,256]{0,1:T(8,128)S(1)}, u32[]{:S(2)}, u32[]{:S(2)}) collective-permute-start(f32[384,256]{0,1:T(8,128)S(1)} %fusion.29), channel_id=1, source_target_pairs={{0,1},{1,0},{2,3},{3,2},{4,5},{5,4},{6,7},{7,6},{8,9},{9,8},{10,11... | collective-permute-start | bytes 1179656 | tf_op jit(solution)/shard_map/ppermute | solution.py:47
  178.2 7.4 %collective-permute-start.30 = (f32[96,256]{0,1:T(8,128)S(1)}, f32[96,256]{0,1:T(8,128)S(1)}, u32[]{:S(2)}, u32[]{:S(2)}) collective-permute-start(f32[96,256]{0,1:T(8,128)S(1)} %get-tuple-element.25), channel_id=1, source_target_pairs={{0,16},{8,24},{16,0},{24,8},{1,17},{9,25},{17,1},{25,9},{2,18},{10... | collective-permute-start | bytes 294920 | tf_op jit(solution)/shard_map/ppermute | solution.py:44
  185.6 1.9 collective-permute-start.31
  187.4 4.1 %collective-permute-done.30 = f32[96,256]{0,1:T(8,128)S(1)} collective-permute-done((f32[96,256]{0,1:T(8,128)S(1)}, f32[96,256]{0,1:T(8,128)S(1)}, u32[]{:S(2)}, u32[]{:S(2)}) %collective-permute-start.30) | collective-permute-done | bytes 98336 | tf_op jit(solution)/shard_map/ppermute | solution.py:44
  193.7 2.6 %collective-permute-start.34 = (f32[96,256]{0,1:T(8,128)S(1)}, f32[96,256]{0,1:T(8,128)S(1)}, u32[]{:S(2)}, u32[]{:S(2)}) collective-permute-start(f32[96,256]{0,1:T(8,128)S(1)} %add_add_fusion.1), channel_id=1, source_target_pairs={{0,6},{1,7},{2,4},{3,5},{4,2},{5,3},{6,0},{7,1},{8,14},{9,15},{10,... | collective-permute-start | bytes 294920 | tf_op jit(solution)/shard_map/ppermute | solution.py:50
  197.1 7.3 %collective-permute-done.33 = f32[96,256]{0,1:T(8,128)S(1)} collective-permute-done((f32[96,256]{0,1:T(8,128)S(1)}, f32[96,256]{0,1:T(8,128)S(1)}, u32[]{:S(2)}, u32[]{:S(2)}) %collective-permute-start.33) | collective-permute-done | bytes 98336 | tf_op jit(solution)/shard_map/ppermute | solution.py:50
  209.3 3.5 %collective-permute-done.35 = f32[96,256]{0,1:T(8,128)S(1)} collective-permute-done((f32[96,256]{0,1:T(8,128)S(1)}, f32[96,256]{0,1:T(8,128)S(1)}, u32[]{:S(2)}, u32[]{:S(2)}) %collective-permute-start.35) | collective-permute-done | bytes 98336 | tf_op jit(solution)/shard_map/ppermute | solution.py:44
  (156 shorter events, 87.1 us)
Async XLA Ops:
  2.9 14.4 %collective-permute-start.1 = (f32[384,256]{0,1:T(8,128)S(1)}, f32[384,256]{0,1:T(8,128)S(1)}, u32[]{:S(2)}, u32[]{:S(2)}) collective-permute-start(f32[384,256]{0,1:T(8,128)S(1)} %bitcast_multiply_fusion.1), channel_id=1, source_target_pairs={{0,2},{1,3},{2,4},{3,5},{4,6},{5,7},{8,10},{9,11},{10,12},{11,13},... | collective-permute-start | bytes 1179656 | tf_op jit(solution)/shard_map/ppermute | solution.py:54
  9.0 15.6 %collective-permute-start.15 = (f32[384,256]{0,1:T(8,128)S(1)}, f32[384,256]{0,1:T(8,128)S(1)}, u32[]{:S(2)}, u32[]{:S(2)}) collective-permute-start(f32[384,256]{0,1:T(8,128)S(1)} %bitcast_multiply_fusion), channel_id=1, source_target_pairs={{0,2},{1,3},{2,4},{3,5},{4,6},{5,7},{8,10},{9,11},{10,12},{11,13},... | collective-permute-start | bytes 1179656 | tf_op jit(solution)/shard_map/ppermute | solution.py:54
  12.5 14.0 %collective-permute-start.18 = (f32[384,256]{0,1:T(8,128)S(1)}, f32[384,256]{0,1:T(8,128)}, u32[]{:S(2)}, u32[]{:S(2)}) collective-permute-start(f32[384,256]{0,1:T(8,128)S(1)} %bitcast_multiply_fusion), channel_id=1, source_target_pairs={{2,0},{3,1},{4,2},{5,3},{6,4},{7,5},{10,8},{11,9},{12,10},{13,11},... | collective-permute-start | bytes 1179656 | tf_op jit(solution)/shard_map/ppermute | solution.py:58
  13.8 21.1 %collective-permute-start.4 = (f32[384,256]{0,1:T(8,128)S(1)}, f32[384,256]{0,1:T(8,128)}, u32[]{:S(2)}, u32[]{:S(2)}) collective-permute-start(f32[384,256]{0,1:T(8,128)S(1)} %bitcast_multiply_fusion.1), channel_id=1, source_target_pairs={{2,0},{3,1},{4,2},{5,3},{6,4},{7,5},{10,8},{11,9},{12,10},{13,11},... | collective-permute-start | bytes 1179656 | tf_op jit(solution)/shard_map/ppermute | solution.py:58
  17.3 18.9 %collective-permute-start.2 = (f32[384,256]{0,1:T(8,128)S(1)}, f32[384,256]{0,1:T(8,128)}, u32[]{:S(2)}, u32[]{:S(2)}) collective-permute-start(f32[384,256]{0,1:T(8,128)S(1)} %collective-permute-done.1), channel_id=1, source_target_pairs={{2,4},{3,5},{4,6},{5,7},{10,12},{11,13},{12,14},{13,15},{18,20},{1... | collective-permute-start | bytes 1179656 | tf_op jit(solution)/shard_map/ppermute | solution.py:54
  18.7 36.0 %collective-permute-start = (f32[384,256]{0,1:T(8,128)S(1)}, f32[384,256]{0,1:T(8,128)S(1)}, u32[]{:S(2)}, u32[]{:S(2)}) collective-permute-start(f32[384,256]{0,1:T(8,128)S(1)} %bitcast_multiply_fusion.1), channel_id=1, source_target_pairs={{0,1},{1,0},{2,3},{3,2},{4,5},{5,4},{6,7},{7,6},{8,9},{9,8},{10,11... | collective-permute-start | bytes 1179656 | tf_op jit(solution)/shard_map/ppermute | solution.py:47
  24.6 13.9 %collective-permute-start.16 = (f32[384,256]{0,1:T(8,128)S(1)}, f32[384,256]{0,1:T(8,128)S(1)}, u32[]{:S(2)}, u32[]{:S(2)}) collective-permute-start(f32[384,256]{0,1:T(8,128)S(1)} %collective-permute-done.15), channel_id=1, source_target_pairs={{2,4},{3,5},{4,6},{5,7},{10,12},{11,13},{12,14},{13,15},{18,20},{1... | collective-permute-start | bytes 1179656 | tf_op jit(solution)/shard_map/ppermute | solution.py:54
  26.5 17.4 %collective-permute-start.20 = (f32[384,256]{0,1:T(8,128)}, f32[384,256]{0,1:T(8,128)S(1)}, u32[]{:S(2)}, u32[]{:S(2)}) collective-permute-start(f32[384,256]{0,1:T(8,128)} %collective-permute-done.18), channel_id=1, source_target_pairs={{2,0},{3,1},{4,2},{5,3},{10,8},{11,9},{12,10},{13,11},{18,16},{19,... | collective-permute-start | bytes 1179656 | tf_op jit(solution)/shard_map/ppermute | solution.py:58
  34.9 17.4 %collective-permute-start.6 = (f32[384,256]{0,1:T(8,128)}, f32[384,256]{0,1:T(8,128)S(1)}, u32[]{:S(2)}, u32[]{:S(2)}) collective-permute-start(f32[384,256]{0,1:T(8,128)} %collective-permute-done.4), channel_id=1, source_target_pairs={{2,0},{3,1},{4,2},{5,3},{10,8},{11,9},{12,10},{13,11},{18,16},{19,... | collective-permute-start | bytes 1179656 | tf_op jit(solution)/shard_map/ppermute | solution.py:58
  36.2 17.3 %collective-permute-start.3 = (f32[384,256]{0,1:T(8,128)}, f32[384,256]{0,1:T(8,128)S(1)}, u32[]{:S(2)}, u32[]{:S(2)}) collective-permute-start(f32[384,256]{0,1:T(8,128)} %collective-permute-done.2), channel_id=1, source_target_pairs={{4,6},{5,7},{12,14},{13,15},{20,22},{21,23},{28,30},{29,31}} | collective-permute-start | bytes 1179656 | tf_op jit(solution)/shard_map/ppermute | solution.py:54
  38.6 19.5 %collective-permute-start.17 = (f32[384,256]{0,1:T(8,128)S(1)}, f32[384,256]{0,1:T(8,128)S(1)}, u32[]{:S(2)}, u32[]{:S(2)}) collective-permute-start(f32[384,256]{0,1:T(8,128)S(1)} %collective-permute-done.16), channel_id=1, source_target_pairs={{4,6},{5,7},{12,14},{13,15},{20,22},{21,23},{28,30},{29,31}} | collective-permute-start | bytes 1179656 | tf_op jit(solution)/shard_map/ppermute | solution.py:54
  43.8 16.9 %collective-permute-start.22 = (f32[384,256]{0,1:T(8,128)S(1)}, f32[384,256]{0,1:T(8,128)S(1)}, u32[]{:S(2)}, u32[]{:S(2)}) collective-permute-start(f32[384,256]{0,1:T(8,128)S(1)} %collective-permute-done.20), channel_id=1, source_target_pairs={{2,0},{3,1},{10,8},{11,9},{18,16},{19,17},{26,24},{27,25}} | collective-permute-start | bytes 1179656 | tf_op jit(solution)/shard_map/ppermute | solution.py:58
  52.2 15.5 %collective-permute-start.8 = (f32[384,256]{0,1:T(8,128)S(1)}, f32[384,256]{0,1:T(8,128)S(1)}, u32[]{:S(2)}, u32[]{:S(2)}) collective-permute-start(f32[384,256]{0,1:T(8,128)S(1)} %collective-permute-done.6), channel_id=1, source_target_pairs={{2,0},{3,1},{10,8},{11,9},{18,16},{19,17},{26,24},{27,25}} | collective-permute-start | bytes 1179656 | tf_op jit(solution)/shard_map/ppermute | solution.py:58
  54.6 14.2 %collective-permute-start.5 = (f32[384,256]{0,1:T(8,128)S(1)}, f32[384,256]{0,1:T(8,128)S(1)}, u32[]{:S(2)}, u32[]{:S(2)}) collective-permute-start(f32[384,256]{0,1:T(8,128)S(1)} %add.136), channel_id=1, source_target_pairs={{0,1},{1,0},{2,3},{3,2},{4,5},{5,4},{6,7},{7,6},{8,9},{9,8},{10,11... | collective-permute-start | bytes 1179656 | tf_op jit(solution)/shard_map/ppermute | solution.py:47
  56.4 50.4 %collective-permute-start.21 = (f32[384,256]{0,1:T(8,128)S(1)}, f32[384,256]{0,1:T(8,128)}, u32[]{:S(2)}, u32[]{:S(2)}) collective-permute-start(f32[384,256]{0,1:T(8,128)S(1)} %add.148), channel_id=1, source_target_pairs={{0,1},{1,0},{2,3},{3,2},{4,5},{5,4},{6,7},{7,6},{8,9},{9,8},{10,11... | collective-permute-start | bytes 1179656 | tf_op jit(solution)/shard_map/ppermute | solution.py:47
  60.7 41.9 %collective-permute-start.19 = (f32[384,256]{0,1:T(8,128)}, f32[384,256]{0,1:T(8,128)}, u32[]{:S(2)}, u32[]{:S(2)}) collective-permute-start(f32[384,256]{0,1:T(8,128)} %add.147), channel_id=1, source_target_pairs={{0,1},{1,0},{2,3},{3,2},{4,5},{5,4},{6,7},{7,6},{8,9},{9,8},{10,11... | collective-permute-start | bytes 1179656 | tf_op jit(solution)/shard_map/ppermute | solution.py:47
  67.7 41.8 %collective-permute-start.23 = (f32[384,256]{0,1:T(8,128)S(1)}, f32[384,256]{0,1:T(8,128)}, u32[]{:S(2)}, u32[]{:S(2)}) collective-permute-start(f32[384,256]{0,1:T(8,128)S(1)} %add.149), channel_id=1, source_target_pairs={{0,1},{1,0},{2,3},{3,2},{4,5},{5,4},{6,7},{7,6},{8,9},{9,8},{10,11... | collective-permute-start | bytes 1179656 | tf_op jit(solution)/shard_map/ppermute | solution.py:47
  99.6 38.3 %collective-permute-start.10 = (f32[384,256]{0,1:T(8,128)}, f32[384,256]{0,1:T(8,128)}, u32[]{:S(2)}, u32[]{:S(2)}) collective-permute-start(f32[384,256]{0,1:T(8,128)} %get-tuple-element.11), channel_id=1, source_target_pairs={{0,8},{8,0},{16,24},{24,16},{1,9},{9,1},{17,25},{25,17},{2,10},{10... | collective-permute-start | bytes 1179656 | tf_op jit(solution)/shard_map/ppermute | solution.py:44
  101.1 37.3 %collective-permute-start.11 = (f32[384,256]{0,1:T(8,128)}, f32[384,256]{0,1:T(8,128)}, u32[]{:S(2)}, u32[]{:S(2)}) collective-permute-start(f32[384,256]{0,1:T(8,128)} %get-tuple-element.10), channel_id=1, source_target_pairs={{0,16},{8,24},{16,0},{24,8},{1,17},{9,25},{17,1},{25,9},{2,18},{10... | collective-permute-start | bytes 1179656 | tf_op jit(solution)/shard_map/ppermute | solution.py:44
  102.6 35.8 %collective-permute-start.12 = (f32[384,256]{0,1:T(8,128)}, f32[384,256]{0,1:T(8,128)}, u32[]{:S(2)}, u32[]{:S(2)}) collective-permute-start(f32[384,256]{0,1:T(8,128)} %get-tuple-element.9), channel_id=1, source_target_pairs={{0,24},{8,16},{16,8},{24,0},{1,25},{9,17},{17,9},{25,1},{2,26},{10... | collective-permute-start | bytes 1179656 | tf_op jit(solution)/shard_map/ppermute | solution.py:44
  134.8 13.4 %collective-permute-start.24 = (f32[384,256]{0,1:T(8,128)S(1)}, f32[384,256]{0,1:T(8,128)S(1)}, u32[]{:S(2)}, u32[]{:S(2)}) collective-permute-start(f32[384,256]{0,1:T(8,128)S(1)} %get-tuple-element.14), channel_id=1, source_target_pairs={{0,8},{8,0},{16,24},{24,16},{1,9},{9,1},{17,25},{25,17},{2,10},{10... | collective-permute-start | bytes 1179656 | tf_op jit(solution)/shard_map/ppermute | solution.py:44
  136.4 25.8 %collective-permute-start.25 = (f32[384,256]{0,1:T(8,128)S(1)}, f32[384,256]{0,1:T(8,128)S(1)}, u32[]{:S(2)}, u32[]{:S(2)}) collective-permute-start(f32[384,256]{0,1:T(8,128)S(1)} %get-tuple-element.13), channel_id=1, source_target_pairs={{0,16},{8,24},{16,0},{24,8},{1,17},{9,25},{17,1},{25,9},{2,18},{10... | collective-permute-start | bytes 1179656 | tf_op jit(solution)/shard_map/ppermute | solution.py:44
  137.9 25.6 %collective-permute-start.26 = (f32[384,256]{0,1:T(8,128)S(1)}, f32[384,256]{0,1:T(8,128)S(1)}, u32[]{:S(2)}, u32[]{:S(2)}) collective-permute-start(f32[384,256]{0,1:T(8,128)S(1)} %get-tuple-element.12), channel_id=1, source_target_pairs={{0,24},{8,16},{16,8},{24,0},{1,25},{9,17},{17,9},{25,1},{2,26},{10... | collective-permute-start | bytes 1179656 | tf_op jit(solution)/shard_map/ppermute | solution.py:44
  139.8 26.2 %collective-permute-start.13 = (f32[384,256]{0,1:T(8,128)S(1)}, f32[384,256]{0,1:T(8,128)S(1)}, u32[]{:S(2)}, u32[]{:S(2)}) collective-permute-start(f32[384,256]{0,1:T(8,128)S(1)} %fusion.5), channel_id=1, source_target_pairs={{0,0},{1,4},{2,8},{3,12},{4,16},{5,20},{6,24},{7,28},{8,1},{9,5},{... | collective-permute-start | bytes 1179656 | tf_op jit(solution)/shard_map/ppermute | solution.py:65
  (25 other events, 625.8 us)
